TPU v7x, 256 devices: a whole 4x4x8 slice. The times are simulated.
256 devices in a mesh: dp: 8 (over x, core), space: 32 (over y, z).
Axes of the slice: x: 4, y: 4, z: 8, core: 2. Of those that a mesh axis runs over, the one named last changes fastest.
Arguments:
- features: bfloat16 [8, 262144, 128], P('dp', 'space'), may hold values from -6 to 6
- child_parent: int32 [8, 262144], P('dp', 'space'), may hold values from 0 to 65535, as said below
- child_code: int32 [8, 262144], P('dp', 'space'), may hold values from 0 to 7
- weight: bfloat16 [8, 128, 128], replicated, may hold values from -0.25 to 0.25
- out_grad: bfloat16 [8, 65536, 128], P('dp', 'space'), may hold values from -6 to 6
Outputs:
- parent_out: bfloat16 [8, 65536, 128], P('dp', 'space')
- feature_grad: bfloat16 [8, 262144, 128], P('dp', 'space')
- weight_grad: float32 [8, 128, 128], replicated
Inputs may be any that keep to these rules, and one draw needn't show every extreme that they name: Within one window, child_parent is nondecreasing along the 8192 rows of one device of space. Parent p lies on device p // 2048 of space; at most 512 rows of one device have their parent on one device, and on every device some device receives exactly 512. No two fine octants of a window share both parent and child_code.
All inputs are finite; a program needn't handle non-finite values.
Results may differ from a plain program's by a relative error of at most 0.001.
Values may be sent and summed in bfloat16 or wider, within the bound.
A program may use at most 128 MiB of HBM per device.

v0:
```python
import jax
import jax.numpy as jnp
from jax import lax
from jax.sharding import PartitionSpec as P


def gather_blocks(rows, starts, capacity):
    extended = jnp.concatenate([rows, jnp.zeros((capacity,) + rows.shape[1:], rows.dtype)], axis=0)

    def window(offset):
        return lax.dynamic_slice_in_dim(extended, offset, capacity, 0)

    return jax.vmap(window)(starts)


def spread_blocks(blocks, starts, row_count):
    capacity = blocks.shape[1]
    channels = blocks.shape[2]
    canvas = jnp.zeros((row_count + capacity, channels), blocks.dtype)
    numbers = lax.ScatterDimensionNumbers(
        update_window_dims=(1, 2), inserted_window_dims=(), scatter_dims_to_operand_dims=(0,)
    )
    placed = lax.scatter_add(canvas, starts[:, None], blocks, numbers)
    return placed[:row_count]


def per_device(features, child_parent, child_code, weight, out_grad):
    fine_rows = features[0]
    parents = child_parent[0]
    child_kinds = child_code[0]
    cotangent = out_grad[0]
    row_count = fine_rows.shape[0]
    par_rows = cotangent.shape[0]
    kinds_total = weight.shape[0]
    chan_in = weight.shape[1]
    chan_out = weight.shape[2]
    space_size = lax.axis_size("space")
    capacity = 2 * row_count // space_size
    owners = parents // par_rows
    local_slot = (parents - owners * par_rows) * kinds_total + child_kinds
    counts = jnp.sum((owners[:, None] == jnp.arange(space_size)[None, :]).astype(jnp.int32), axis=0)
    starts = jnp.cumsum(counts) - counts
    slot_lane = jnp.arange(capacity)
    live_mask = slot_lane[None, :] < counts[:, None]
    marker = kinds_total * par_rows
    slot_blocks = gather_blocks(local_slot[:, None], starts, capacity)[:, :, 0]
    send_slots = jnp.where(live_mask, slot_blocks, marker)
    block_rows = min(512, row_count)
    block_count = row_count // block_rows
    kind_onehot = (child_kinds[:, None] == jnp.arange(kinds_total)[None, :]).astype(jnp.bfloat16)
    weight_cat = jnp.transpose(weight, (1, 0, 2)).reshape(chan_in, kinds_total * chan_out)
    weight_back = jnp.transpose(weight, (2, 0, 1)).reshape(chan_out, kinds_total * chan_in)
    rows_blocked = fine_rows.reshape(block_count, block_rows, chan_in)
    onehot_blocked = kind_onehot.reshape(block_count, block_rows, kinds_total)

    def forward_block(packed):
        rows, onehot = packed
        widened = jnp.dot(rows, weight_cat, preferred_element_type=jnp.float32).reshape(
            block_rows, kinds_total, chan_out
        )
        return jnp.sum(widened * onehot.astype(jnp.float32)[:, :, None], axis=1)

    products = lax.map(forward_block, (rows_blocked, onehot_blocked)).reshape(row_count, chan_out)
    part_blocks = gather_blocks(products, starts, capacity)
    send_parts = jnp.where(live_mask[:, :, None], part_blocks, 0.0)
    recv_parts, recv_slots = (
        lax.all_to_all(send_parts, "space", split_axis=0, concat_axis=0, tiled=True),
        lax.all_to_all(send_slots, "space", split_axis=0, concat_axis=0, tiled=True),
    )
    recv_parent = recv_slots // kinds_total
    summed = (
        jnp.zeros((par_rows, chan_out), jnp.float32)
        .at[recv_parent.reshape(-1)]
        .add(recv_parts.reshape(-1, chan_out), mode="drop")
    )
    result = summed.astype(jnp.bfloat16)
    back_rows = jnp.take(cotangent, recv_parent, axis=0, mode="fill", fill_value=0)
    returned = lax.all_to_all(back_rows, "space", split_axis=0, concat_axis=0, tiled=True)
    child_cot = spread_blocks(returned, starts, row_count)
    cot_blocked = child_cot.reshape(block_count, block_rows, chan_out)

    def backward_block(carry, packed):
        rows, onehot, cot = packed
        widened = jnp.dot(cot, weight_back, preferred_element_type=jnp.float32).reshape(
            block_rows, kinds_total, chan_in
        )
        grads = jnp.sum(widened * onehot.astype(jnp.float32)[:, :, None], axis=1).astype(
            jnp.bfloat16
        )
        placed = (rows[:, None, :] * onehot[:, :, None]).reshape(block_rows, kinds_total * chan_in)
        carry = carry + lax.dot_general(
            placed, cot, (((0,), (0,)), ((), ())), preferred_element_type=jnp.float32
        )
        return (carry, grads)

    start_term = jnp.zeros((kinds_total * chan_in, chan_out), jnp.float32)
    weight_term, grad_blocks = lax.scan(
        backward_block, start_term, (rows_blocked, onehot_blocked, cot_blocked)
    )
    feature_grad = grad_blocks.reshape(row_count, chan_in)
    summed_terms = lax.psum(weight_term, ("dp", "space"))
    total_rows = row_count * space_size * lax.axis_size("dp")
    weight_grad = (summed_terms / jnp.sqrt(jnp.float32(total_rows))).reshape(
        kinds_total, chan_in, chan_out
    )
    return (result[None], feature_grad[None], weight_grad)


def solution(mesh):
    placed = (
        P("dp", "space", None),
        P("dp", "space"),
        P("dp", "space"),
        P(),
        P("dp", "space", None),
    )
    return jax.shard_map(
        per_device,
        mesh=mesh,
        in_specs=placed,
        out_specs=(P("dp", "space", None), P("dp", "space", None), P()),
        check_vma=False,
    )
```

profile of v0, /device:TPU:2, one launch (start us, length us, event | category | flops | bytes accessed | tf_op | source)
XLA Modules:
  0.0 933.6 jit_solution(17775273788267957217)
XLA Ops:
  9.6 42.1 %while.32 = (s32[]{:T(128)}, s32[8704,1]{0,1:T(1,128)S(1)}, s32[32,2]{0,1:T(2,128)S(1)}, s32[32,512,1]{1,2,0:T(1,128)S(1)}) while((s32[]{:T(128)}, s32[8704,1]{0,1:T(1,128)S(1)}, s32[32,2]{0,1:T(2,128)S(1)}, s32[32,512,1]{1,2,0:T(1,128)S(1)}) %tuple.98), condition=%wide.while_cond.clone, body=%wide.while_body.sunk.clone | while | flops 2 | bytes 4193 | solution.py:11
  52.4 11.5 %all-to-all-start = ((s32[32,1,512]{2,1,0:T(1,128)}), s32[32,1,512]{2,1,0:T(1,128)S(1)}, u32[]{:S(2)}, u32[]{:S(2)}) async-start(s32[32,1,512]{2,1,0:T(1,128)} %compare_select_fusion.2), calls=%async_computation | async-start | bytes 131072 | tf_op jit(solution)/shard_map/all_to_all | solution.py:68
  67.1 37.0 %while.31 = (s32[]{:T(128)}, f32[16,512,128]{2,1,0:T(8,128)}, bf16[16,512,128]{2,1,0:T(8,128)(2,1)}, bf16[128,1024]{0,1:T(8,128)(2,1)S(1)}, bf16[16,512,8]{1,2,0:T(8,128)(2,1)S(1)}) while((s32[]{:T(128)}, f32[16,512,128]{2,1,0:T(8,128)}, bf16[16,512,128]{2,1,0:T(8,128)(2,1)}, bf16[128,1024]{0,1:T(8,128)(2,1)S(1)}, ...), condition=%wide.region_4.5_spmd.clone, body=%wide.region_2.4_spmd.sunk.clone | while | flops 135204864 | bytes 1220689 | solution.py:63
  104.5 57.4 %gather_fusion = bf16[16384,128]{1,0:T(8,128)(2,1)} fusion(bf16[2048,128]{1,0:T(8,128)(2,1)S(1)} %bitcast.167, s32[16384]{0:T(1024)S(1)} %broadcast_clamp_fusion), kind=kCustom, calls=%fused_computation | custom fusion | bytes 8454144 | tf_op jit(solution)/shard_map/jit(_take)/gather | solution.py:77
  161.9 7.7 broadcast_select_fusion.1
  169.6 9.9 %all-to-all-start.2 = ((bf16[32,512,128]{2,1,0:T(8,128)(2,1)}), bf16[32,512,128]{2,1,0:T(8,128)(2,1)}, u32[]{:S(2)}, u32[]{:S(2)}) async-start(bf16[32,512,128]{2,1,0:T(8,128)(2,1)} %broadcast_select_fusion.1), calls=%async_computation.2 | async-start | bytes 8388608 | tf_op jit(solution)/shard_map/all_to_all | solution.py:78
  179.6 3.8 concatenate.12
  183.4 93.2 %while.33 = (s32[]{:T(128)}, f32[8704,128]{1,0:T(8,128)}, s32[32,2]{0,1:T(2,128)S(1)}, f32[32,512,128]{2,1,0:T(8,128)}) while((s32[]{:T(128)}, f32[8704,128]{1,0:T(8,128)}, s32[32,2]{0,1:T(2,128)S(1)}, f32[32,512,128]{2,1,0:T(8,128)}) %tuple.121), condition=%wide.while_cond.1.clone, body=%wide.while_body.1.sunk.clone | while | flops 2 | bytes 524893 | solution.py:11
  184.0 2.3 bitcast_dynamic-update-slice_fusion.14
  189.9 2.3 bitcast_dynamic-update-slice_fusion.14
  201.5 2.3 bitcast_dynamic-update-slice_fusion.14
  207.3 2.3 bitcast_dynamic-update-slice_fusion.14
  213.2 2.3 bitcast_dynamic-update-slice_fusion.14
  233.5 2.3 bitcast_dynamic-update-slice_fusion.14
  236.4 2.3 bitcast_dynamic-update-slice_fusion.14
  256.8 2.3 bitcast_dynamic-update-slice_fusion.14
  259.7 2.3 bitcast_dynamic-update-slice_fusion.14
  274.3 2.3 bitcast_dynamic-update-slice_fusion.14
  276.6 9.9 %broadcast_select_fusion = f32[32,512,128]{2,1,0:T(8,128)} fusion(f32[32,512,128]{2,1,0:T(8,128)} %get-tuple-element.86, pred[32,512]{1,0:T(8,128)(4,1)S(1)} %iota_compare_fusion.2), kind=kLoop, calls=%fused_computation.28 | loop fusion | flops 2097152 | bytes 16793600 | tf_op jit(solution)/shard_map/jit(_where)/select_n | solution.py:65
  286.5 10.0 %all-to-all-start.1 = ((f32[32,512,128]{2,1,0:T(8,128)}), f32[32,512,128]{2,1,0:T(8,128)}, u32[]{:S(2)}, u32[]{:S(2)}) async-start(f32[32,512,128]{2,1,0:T(8,128)} %broadcast_select_fusion), calls=%async_computation.1 | async-start | bytes 16777216 | tf_op jit(solution)/shard_map/all_to_all | solution.py:67
  296.9 177.0 %while.34 = (s32[]{:T(128)}, bf16[8704,128]{1,0:T(8,128)(2,1)S(1)}, s32[32]{0:T(128)S(1)}, bf16[32,512,128]{2,1,0:T(8,128)(2,1)}, s32[2]{0:T(128)S(1)}, /*index=5*/s32[1]{0:T(128)}) while((s32[]{:T(128)}, bf16[8704,128]{1,0:T(8,128)(2,1)S(1)}, s32[32]{0:T(128)S(1)}, bf16[32,512,128]{2,1,0:T(8,128)(2,1)}, s32[2]{0:T(128)S(1)}, ...), condition=%wide.while_cond.2.clone, body=%wide.while_body.2.sunk.clone | while | flops 327691 | bytes 655479 | solution.py:23
  475.4 102.7 %while.35 = (s32[]{:T(128)}, f32[1024,128]{1,0:T(8,128)S(1)}, bf16[16,512,128]{2,1,0:T(8,128)(2,1)}, bf16[16,512,128]{2,1,0:T(8,128)(2,1)}, bf16[16,512,8]{1,2,0...) while((s32[]{:T(128)}, f32[1024,128]{1,0:T(8,128)S(1)}, ...), condition=%wide.region_9.10_spmd.clone.clone, body=%wide.region_7.9_spmd.clone.sunk.clone | while | flops 270209024 | bytes 4530291 | solution.py:97
  579.3 256.9 %all-reduce.5.cloned.1.call-done = f32[1024,128]{1,0:T(8,128)} async-done(((f32[1024,128]{1,0:T(8,128)}), f32[1024,128]{1,0:T(8,128)}) %all-reduce.5.cloned.1.call-update) | async-done | bytes 524304 | tf_op jit(solution)/shard_map/psum | solution.py:101
  838.0 87.9 %scatter_custom_fusion = f32[2048,128]{1,0:T(8,128)S(1)} fusion(s32[16384]{0:T(1024)S(1)} %bitcast.182, f32[16384,128]{1,0:T(8,128)} %bitcast.17, f32[]{:T(128)} %constant.60.clone.1), kind=kCustom, calls=%fused_computation.33 | custom fusion | flops 2097152 | bytes 1049088 | tf_op jit(solution)/shard_map/scatter-add | solution.py:74
  (512 shorter events, 439.5 us)
Async XLA Ops:
  7.2 97.3 %copy-start = (bf16[1,2048,128]{2,1,0:T(8,128)(2,1)S(1)}, bf16[1,2048,128]{2,1,0:T(8,128)(2,1)}, u32[]{:S(2)}) copy-start(bf16[1,2048,128]{2,1,0:T(8,128)(2,1)} %param.13) | copy-start | bytes 1572868
  52.4 51.7 %all-to-all-start = ((s32[32,1,512]{2,1,0:T(1,128)}), s32[32,1,512]{2,1,0:T(1,128)S(1)}, u32[]{:S(2)}, u32[]{:S(2)}) async-start(s32[32,1,512]{2,1,0:T(1,128)} %compare_select_fusion.2), calls=%async_computation | async-start | bytes 131072 | tf_op jit(solution)/shard_map/all_to_all | solution.py:68
  104.1 57.8 %copy-start.2 = (bf16[16,512,8]{1,2,0:T(8,128)(2,1)}, bf16[16,512,8]{1,2,0:T(8,128)(2,1)S(1)}, u32[]{:S(2)}) copy-start(bf16[16,512,8]{1,2,0:T(8,128)(2,1)S(1)} %get-tuple-element.503) | copy-start | bytes 393220
  169.6 116.9 %all-to-all-start.2 = ((bf16[32,512,128]{2,1,0:T(8,128)(2,1)}), bf16[32,512,128]{2,1,0:T(8,128)(2,1)}, u32[]{:S(2)}, u32[]{:S(2)}) async-start(bf16[32,512,128]{2,1,0:T(8,128)(2,1)} %broadcast_select_fusion.1), calls=%async_computation.2 | async-start | bytes 8388608 | tf_op jit(solution)/shard_map/all_to_all | solution.py:78
  286.5 10.4 %copy-start.3 = (s32[2]{0:T(128)S(1)}, s32[2]{0:T(128)}, u32[]{:S(2)}) copy-start(s32[2]{0:T(128)} %constant.226) | copy-start | bytes 28
  286.5 551.5 %all-to-all-start.1 = ((f32[32,512,128]{2,1,0:T(8,128)}), f32[32,512,128]{2,1,0:T(8,128)}, u32[]{:S(2)}, u32[]{:S(2)}) async-start(f32[32,512,128]{2,1,0:T(8,128)} %broadcast_select_fusion), calls=%async_computation.1 | async-start | bytes 16777216 | tf_op jit(solution)/shard_map/all_to_all | solution.py:67
  296.5 539.6 %all-reduce.5.cloned.1.call-start = ((), (), s32[]{:S(2)}) async-start(), calls=%async_computation.3 | async-start | bytes 1048576 | tf_op jit(solution)/shard_map/psum | solution.py:101
  578.1 0.8 copy-start.1
Sparse Core Ops, SparseCore 0:
  579.0 257.0 all-reduce.4
where the time goes:
time: 940 us; the launch traced here: 934 us
  local copies, waits for them, and re-layouts  298 us (32%)
  waiting for transfers between devices  257 us (27%)
  other arithmetic  255 us (27%)
  matrix products  76.7 us (8%)
  starting transfers between devices  31.4 us (3%)
  between operations  14.2 us (2%)
    psum x1, waiting for transfers between devices, per_device(): summed_terms = lax.psum(weight_term, ('dp', 'space'))  257 us
    gather x192, local copies, waits for them, and re-layouts  135 us
    scatter-add x64, other arithmetic  119 us
    scatter-add x1, other arithmetic, per_device(): summed = jnp.zeros((par_rows, chan_out), jnp.float32).at[recv_parent.resh...  87.9 us
    gather x1, local copies, waits for them, and re-layouts, per_device(): jnp.take(cotangent, recv_parent, axis=0, mode='fill', fill_value=0)  57.4 us
    scatter-add x64, local copies, waits for them, and re-layouts  57.4 us
    dot_general x16, matrix products, backward_block(): jnp.dot(cot, weight_back, preferred_element_type=jnp.float32)  26.9 us
    dot_general x16, matrix products, forward_block(): jnp.dot(rows, weight_cat, preferred_element_type=jnp.float32)  25 us
  transfers between devices with their start and end apart: 4, of which 1 were waited for; matrix products, arithmetic and copies ran while one was open for 46% of the time, Pallas kernels for 0%

commit v1 on v0

v1 whole, which is shorter than its diff:
```python
import jax
import jax.numpy as jnp
from jax import lax
from jax.experimental import pallas as pl
from jax.experimental.pallas import tpu as pltpu
from jax.sharding import PartitionSpec as P

MESH = pl.DeviceIdType.MESH
NY = 4
NZ = 8
NS = NY * NZ
ND = 8
CAP = 528
KINDS = 8
PAR = 2048
SLOTS = KINDS * PAR
F32 = jnp.float32
BF16 = jnp.bfloat16
I32 = jnp.int32
ANY = pl.BlockSpec(memory_space=pl.ANY)
VM = pl.BlockSpec(memory_space=pltpu.VMEM)
SM = pl.BlockSpec(memory_space=pltpu.SMEM)
VLIM = 60 * 1024 * 1024


def pack_kernel(first_ref, lo_ref, hi_ref, feat_ref, slot_ref, row_ref, blk_ref, slots_ref, rows_ref):
    d = pl.program_id(0)
    first = pl.multiple_of(first_ref[d], 16)
    lo, hi = lo_ref[d], hi_ref[d]
    blk_ref[0] = feat_ref[pl.ds(first, CAP), :]
    at, lane0 = first // 128, lax.rem(first, 128)
    turn = lax.rem(128 - lane0, 128)
    lane = lax.broadcasted_iota(I32, (8, 128), 1)
    pos = lax.broadcasted_iota(I32, (8, 128), 0) * 128 + lane
    live = (pos >= lo) & (pos < hi)
    for src, dst, marker in ((slot_ref, slots_ref, SLOTS), (row_ref, rows_ref, 0)):
        here = pltpu.roll(src[pl.ds(at, 8), :], turn, 1)
        after = pltpu.roll(src[pl.ds(at + 1, 8), :], turn, 1)
        moved = jnp.where(lane < 128 - lane0, here, after)
        moved = jnp.where(live, moved, marker)
        moved = jnp.where(pos == 1022, lo, jnp.where(pos == 1023, hi, moved))
        dst[0] = moved


def pack(first, lo, hi, feats, slot2d, row2d):
    rows = feats.shape[0]
    return pl.pallas_call(
        pack_kernel,
        out_shape=(
            jax.ShapeDtypeStruct((NS, CAP, 128), BF16),
            jax.ShapeDtypeStruct((NS, 8, 128), I32),
            jax.ShapeDtypeStruct((NS, 8, 128), I32),
        ),
        grid=(NS,),
        in_specs=[
            SM,
            SM,
            SM,
            pl.BlockSpec((rows, 128), lambda d: (0, 0)),
            pl.BlockSpec(slot2d.shape, lambda d: (0, 0)),
            pl.BlockSpec(row2d.shape, lambda d: (0, 0)),
        ],
        out_specs=(
            pl.BlockSpec((1, CAP, 128), lambda d: (d, 0, 0)),
            pl.BlockSpec((1, 8, 128), lambda d: (d, 0, 0)),
            pl.BlockSpec((1, 8, 128), lambda d: (d, 0, 0)),
        ),
        name="pack",
    )(first, lo, hi, feats, slot2d, row2d)


def exchange_kernel(grad_ref, rows_ref, slots_ref, table_ref, want_ref, got_ref, ss, rs, ys, yr, gs, gr, local):
    dp, me = lax.axis_index("dp"), lax.axis_index("space")
    y, z = me // NZ, lax.rem(me, NZ)
    barrier = pltpu.get_barrier_semaphore()

    def greet(i, c):
        pl.semaphore_signal(barrier, inc=1, device_id=(dp, lax.rem(me + i, NS)), device_id_type=MESH)
        return c

    lax.fori_loop(1, NS, greet, 0)
    pl.semaphore_wait(barrier, NS - 1)

    def slots_to(i):
        t = lax.rem(me + i, NS)
        return pltpu.make_async_remote_copy(
            slots_ref.at[t], got_ref.at[me], gs.at[i], gr.at[i], device_id=(dp, t), device_id_type=MESH
        )

    def rows_to(i):
        ty = lax.rem(y + i, NY)
        return pltpu.make_async_remote_copy(
            rows_ref.at[ty], want_ref.at[y], ys.at[i], yr.at[i], device_id=(dp, ty * NZ + z), device_id_type=MESH
        )

    own = [
        pltpu.make_async_copy(grad_ref, table_ref.at[z], local.at[0]),
        pltpu.make_async_copy(rows_ref.at[y], want_ref.at[y], local.at[1]),
        pltpu.make_async_copy(slots_ref.at[me], got_ref.at[me], local.at[2]),
    ]
    half = PAR // 2

    def hop(k, side):
        block = lax.rem(z - k + NZ, NZ) if side == 0 else lax.rem(z + k, NZ)
        to = lax.rem(z + 1, NZ) if side == 0 else lax.rem(z + NZ - 1, NZ)
        part = pl.ds(0, PAR) if k < 3 else pl.ds(side * half, half)
        src = grad_ref.at[part] if k == 0 else table_ref.at[block, part]
        return pltpu.make_async_remote_copy(
            src,
            table_ref.at[block, part],
            ss.at[side, k],
            rs.at[side, k],
            device_id=(dp, y * NZ + to),
            device_id_type=MESH,
        )

    hops = [[hop(k, side) for side in range(2)] for k in range(4)]
    for side in range(2):
        hops[0][side].start()
    for i in range(1, NY):
        rows_to(i).start()

    def start_slots(i, c):
        slots_to(i).start()
        return c

    lax.fori_loop(1, NS, start_slots, 0)
    for copy in own:
        copy.start()
    for k in range(1, 4):
        for side in range(2):
            hops[k - 1][side].wait_recv()
            hops[k][side].start()
    for side in range(2):
        hops[3][side].wait_recv()
    for k in range(4):
        for side in range(2):
            hops[k][side].wait_send()
    for i in range(1, NY):
        rows_to(i).wait()

    def end_slots(i, c):
        slots_to(i).wait()
        return c

    lax.fori_loop(1, NS, end_slots, 0)
    for copy in own:
        copy.wait()


def exchange(grad, rows, slots):
    return pl.pallas_call(
        exchange_kernel,
        out_shape=(
            jax.ShapeDtypeStruct((NZ, PAR, 128), BF16),
            jax.ShapeDtypeStruct(rows.shape, I32),
            jax.ShapeDtypeStruct(slots.shape, I32),
        ),
        in_specs=[ANY] * 3,
        out_specs=(ANY,) * 3,
        scratch_shapes=[
            pltpu.SemaphoreType.DMA((2, 4)),
            pltpu.SemaphoreType.DMA((2, 4)),
            pltpu.SemaphoreType.DMA((NY,)),
            pltpu.SemaphoreType.DMA((NY,)),
            pltpu.SemaphoreType.DMA((NS,)),
            pltpu.SemaphoreType.DMA((NS,)),
            pltpu.SemaphoreType.DMA((3,)),
        ],
        compiler_params=pltpu.CompilerParams(collective_id=1, has_side_effects=True),
        name="exchange",
    )(grad, rows, slots)


def gather_kernel(want_ref, table_ref, out_ref, wide, rowbuf):
    d = pl.program_id(0)

    @pl.when(d == 0)
    def _():
        def widen(i, c):
            at = pl.ds(pl.multiple_of(i * 512, 512), 512)
            wide[at, :] = table_ref[at, :].astype(F32)
            return c

        lax.fori_loop(0, NZ * PAR // 512, widen, 0)

    base = d * 1024
    lo, hi = want_ref[base + 1022], want_ref[base + 1023]

    def group(g, c):
        for u in range(8):
            j = g * 8 + u
            rowbuf[pl.ds(j, 1), :] = wide[pl.ds(want_ref[base + j], 1), :]
        return c

    lax.fori_loop(lo // 8, (hi + 7) // 8, group, 0)
    out_ref[0] = rowbuf[...].astype(BF16)


def gather(want, table):
    return pl.pallas_call(
        gather_kernel,
        out_shape=jax.ShapeDtypeStruct((NS, CAP, 128), BF16),
        grid=(NS,),
        in_specs=[SM, pl.BlockSpec((NZ * PAR, 128), lambda d: (0, 0))],
        out_specs=pl.BlockSpec((1, CAP, 128), lambda d: (d, 0, 0)),
        scratch_shapes=[pltpu.VMEM((NZ * PAR, 128), F32), pltpu.VMEM((CAP, 128), F32)],
        compiler_params=pltpu.CompilerParams(vmem_limit_bytes=VLIM),
        name="gather",
    )(want, table)


def owner_kernel(slot_ref, blk_ref, weight_ref, grad_ref, out_ref, term_ref, grid_ref, rowbuf):
    d = pl.program_id(0)

    @pl.when(d == 0)
    def _():
        def clear(i, c):
            grid_ref[pl.ds(pl.multiple_of(i * 512, 512), 512), :] = jnp.zeros((512, 128), F32)
            return c

        lax.fori_loop(0, SLOTS // 512, clear, 0)

    rowbuf[...] = blk_ref[0].astype(F32)
    base = d * 1024
    lo, hi = slot_ref[base + 1022], slot_ref[base + 1023]

    def group(g, c):
        for u in range(8):
            j = g * 8 + u
            grid_ref[pl.ds(slot_ref[base + j], 1), :] = rowbuf[pl.ds(j, 1), :]
        return c

    lax.fori_loop(lo // 8, (hi + 7) // 8, group, 0)

    @pl.when(d == NS - 1)
    def _():
        term_ref[...] = jnp.zeros(term_ref.shape, F32)

        def chunk(i, c):
            at = pl.ds(pl.multiple_of(i * 512, 512), 512)
            cot = grad_ref[at, :]
            total = jnp.zeros((512, 128), F32)
            for k in range(KINDS):
                kids = grid_ref[pl.ds(pl.multiple_of(k * PAR + i * 512, 512), 512), :].astype(BF16)
                total = total + jnp.dot(kids, weight_ref[k], preferred_element_type=F32)
                term_ref[k * 128 : (k + 1) * 128, :] += lax.dot_general(
                    kids, cot, (((0,), (0,)), ((), ())), preferred_element_type=F32
                )
            out_ref[at, :] = total.astype(BF16)
            return c

        lax.fori_loop(0, PAR // 512, chunk, 0)


def owner(slots, blocks, weight, grad):
    return pl.pallas_call(
        owner_kernel,
        out_shape=(
            jax.ShapeDtypeStruct((PAR, 128), BF16),
            jax.ShapeDtypeStruct((KINDS * 128, 128), F32),
        ),
        grid=(NS,),
        in_specs=[
            SM,
            pl.BlockSpec((1, CAP, 128), lambda d: (d, 0, 0)),
            pl.BlockSpec((KINDS, 128, 128), lambda d: (0, 0, 0)),
            pl.BlockSpec((PAR, 128), lambda d: (0, 0)),
        ],
        out_specs=(
            pl.BlockSpec((PAR, 128), lambda d: (0, 0)),
            pl.BlockSpec((KINDS * 128, 128), lambda d: (0, 0)),
        ),
        scratch_shapes=[pltpu.VMEM((SLOTS + 8, 128), F32), pltpu.VMEM((CAP, 128), F32)],
        compiler_params=pltpu.CompilerParams(vmem_limit_bytes=VLIM),
        name="owner",
    )(slots, blocks, weight, grad)


def total_kernel(scale, term_ref, out_ref, b1, s1, b2, s2, b3, s3, b4, s4, send, recv):
    dp, me = lax.axis_index("dp"), lax.axis_index("space")
    y, z = me // NZ, lax.rem(me, NZ)
    at_dp = lambda i: (lax.rem(dp + i, ND), me)
    at_z = lambda i: (dp, y * NZ + lax.rem(z + i, NZ))
    at_y = lambda i: (dp, lax.rem(y + i, NY) * NZ + z)
    barrier = pltpu.get_barrier_semaphore()
    for who, n in ((at_dp, ND), (at_z, NZ), (at_y, NY)):
        for i in range(1, n):
            pl.semaphore_signal(barrier, inc=1, device_id=who(i), device_id_type=MESH)
    pl.semaphore_wait(barrier, ND + NZ + NY - 3)

    def swap(phase, n, who, src, dst):
        copies = [
            pltpu.make_async_remote_copy(
                src(i), dst, send.at[phase, i], recv.at[phase, i], device_id=who(i), device_id_type=MESH
            )
            for i in range(1, n)
        ]
        for c in copies:
            c.start()
        return copies

    def end(copies):
        for c in copies:
            c.wait()

    def rows(i, n):
        return pl.ds(pl.multiple_of(i * n, n), n)

    c = swap(0, ND, at_dp, lambda i: term_ref.at[rows(lax.rem(dp + i, ND), 128)], b1.at[dp])
    b1[dp] = term_ref[rows(dp, 128), :]
    end(c)
    s1[...] = ((b1[0] + b1[1]) + (b1[2] + b1[3])) + ((b1[4] + b1[5]) + (b1[6] + b1[7]))
    c = swap(1, NZ, at_z, lambda i: s1.at[rows(lax.rem(z + i, NZ), 16)], b2.at[z])
    b2[z] = s1[rows(z, 16), :]
    end(c)
    s2[...] = ((b2[0] + b2[1]) + (b2[2] + b2[3])) + ((b2[4] + b2[5]) + (b2[6] + b2[7]))
    c = swap(2, NY, at_y, lambda i: s2, b3.at[y])
    b3[y] = s2[...]
    end(c)
    s3[...] = ((b3[0] + b3[1]) + (b3[2] + b3[3])) * scale
    c = swap(3, NZ, at_z, lambda i: s3, b4.at[rows(z, 16)])
    b4[rows(z, 16), :] = s3[...]
    end(c)
    c = swap(4, ND, at_dp, lambda i: b4, s4.at[rows(dp, 128)])
    s4[rows(dp, 128), :] = b4[...]
    end(c)
    out_ref[...] = s4[...]


def total(term, scale):
    n = KINDS * 128
    return pl.pallas_call(
        lambda *refs: total_kernel(scale, *refs),
        out_shape=jax.ShapeDtypeStruct((n, 128), F32),
        in_specs=[VM],
        out_specs=VM,
        scratch_shapes=[
            pltpu.VMEM((ND, 128, 128), F32),
            pltpu.VMEM((128, 128), F32),
            pltpu.VMEM((NZ, 16, 128), F32),
            pltpu.VMEM((16, 128), F32),
            pltpu.VMEM((NY, 16, 128), F32),
            pltpu.VMEM((16, 128), F32),
            pltpu.VMEM((128, 128), F32),
            pltpu.VMEM((n, 128), F32),
            pltpu.SemaphoreType.DMA((5, 8)),
            pltpu.SemaphoreType.DMA((5, 8)),
        ],
        compiler_params=pltpu.CompilerParams(collective_id=2, has_side_effects=True),
        name="total",
    )(term)


def fine_kernel(first_ref, lo_ref, hi_ref, back_ref, kind_ref, weight_ref, out_ref, cot):
    d = pl.program_id(0)
    first, lo, hi = first_ref[d], lo_ref[d], hi_ref[d]
    row = lax.broadcasted_iota(I32, (16, 128), 0)

    def tile(t, c):
        src = pl.ds(pl.multiple_of(t * 16, 16), 16)
        dst = pl.ds(pl.multiple_of(first + t * 16, 16), 16)
        keep = row + t * 16 < lo
        new, old = back_ref[0, src, :].astype(F32), cot[dst, :].astype(F32)
        cot[dst, :] = jnp.where(keep, old, new).astype(BF16)
        return c

    lax.fori_loop(lo // 16, (hi + 15) // 16, tile, 0)

    @pl.when(d == NS - 1)
    def _():
        def chunk(i, c):
            at = pl.ds(pl.multiple_of(i * 512, 512), 512)
            rows, kinds = cot[at, :], kind_ref[at, :]
            none = jnp.zeros((512, 128), BF16)
            placed = [jnp.where(kinds == k, rows, none) for k in range(KINDS)]
            wide = jnp.concatenate(placed, axis=1)
            out_ref[at, :] = jnp.dot(wide, weight_ref[...], preferred_element_type=F32).astype(BF16)
            return c

        lax.fori_loop(0, cot.shape[0] // 512, chunk, 0)


def fine(first, lo, hi, back, kinds, weight):
    rows = kinds.shape[0]
    return pl.pallas_call(
        fine_kernel,
        out_shape=jax.ShapeDtypeStruct((rows, 128), BF16),
        grid=(NS,),
        in_specs=[
            SM,
            SM,
            SM,
            pl.BlockSpec((1, CAP, 128), lambda d: (d, 0, 0)),
            pl.BlockSpec((rows, 128), lambda d: (0, 0)),
            pl.BlockSpec(weight.shape, lambda d: (0, 0)),
        ],
        out_specs=pl.BlockSpec((rows, 128), lambda d: (0, 0)),
        scratch_shapes=[pltpu.VMEM((rows, 128), BF16)],
        compiler_params=pltpu.CompilerParams(vmem_limit_bytes=VLIM),
        name="fine",
    )(first, lo, hi, back, kinds, weight)


def per_device(features, child_parent, child_code, weight, out_grad):
    feats, parents, codes, cotangent = features[0], child_parent[0], child_code[0], out_grad[0]
    fine_rows = feats.shape[0]
    owners = parents // PAR
    ends = jnp.sum((owners[:, None] <= jnp.arange(NS)[None, :]).astype(I32), axis=0)
    starts = jnp.concatenate([jnp.zeros((1,), I32), ends[:-1]])
    first = jnp.minimum(starts // 16 * 16, fine_rows - CAP)
    lo, hi = starts - first, ends - first
    slot = codes * PAR + lax.rem(parents, PAR)
    table_row = lax.rem(parents, NZ * PAR)
    as2d = lambda v: jnp.pad(v.reshape(fine_rows // 128, 128), ((0, 16), (0, 0)))
    blocks, slots, rows = pack(first, lo, hi, feats, as2d(slot), as2d(table_row))
    arrived = lax.all_to_all(blocks, "space", split_axis=0, concat_axis=0, tiled=True)
    table, want, got = exchange(cotangent, rows.reshape(NY, NZ * 8, 128), slots)
    reply = gather(want.reshape(-1), table.reshape(NZ * PAR, 128))
    columns = [[y * NZ + z for y in range(NY)] for z in range(NZ)]
    back = lax.all_to_all(
        reply.reshape(NY, NZ * CAP, 128), "space", split_axis=0, concat_axis=0, axis_index_groups=columns, tiled=True
    ).reshape(NS, CAP, 128)
    result, term = owner(got.reshape(-1), arrived, weight, cotangent)
    grad_rows = fine_rows * NS * lax.axis_size("dp")
    weight_grad = total(term, float(1.0 / grad_rows**0.5))
    kinds = jnp.broadcast_to(codes[:, None], (fine_rows, 128)).astype(BF16)
    weight_back = jnp.transpose(weight, (0, 2, 1)).reshape(KINDS * 128, 128)
    feature_grad = fine(first, lo, hi, back, kinds, weight_back)
    return result[None], feature_grad[None], weight_grad.reshape(KINDS, 128, 128)


def solution(mesh):
    placed = (P("dp", "space", None), P("dp", "space"), P("dp", "space"), P(), P("dp", "space", None))
    return jax.shard_map(
        per_device,
        mesh=mesh,
        in_specs=placed,
        out_specs=(P("dp", "space", None), P("dp", "space", None), P()),
        check_vma=False,
    )
```

time: 940 us -> 323 us (0.34)
  local copies, waits for them, and re-layouts: 298 us -> 6.18 us
  other arithmetic: 255 us -> 3.98 us
  waiting for transfers between devices: 257 us -> 66.6 us
  Pallas kernels: 0 us -> 181 us
  matrix products: 76.7 us -> 0 us
  blocking collectives: 0 us -> 54.3 us
  starting transfers between devices: 31.4 us -> 5.08 us
  between operations: 14.2 us -> 0.68 us
    psum x1 -> x0, waiting for transfers between devices: 257 us -> none  [per_device(): summed_terms = lax.psum(weight_term, ('dp', 'space'))]
    scatter-add x65 -> x0, other arithmetic: 207 us -> none
    gather x193 -> x0, local copies, waits for them, and re-layouts: 193 us -> none
    pallas_call x0 -> x6, Pallas kernels: none -> 181 us  [the longest x1 56.2 us: exchange(): pl.pallas_call(exchange_kernel, out_shape=(jax.ShapeDtypeStruct((NZ, PAR,...]
    dot_general x48 -> x0, matrix products: 76.7 us -> none  [the longest x16 26.9 us: backward_block(): jnp.dot(cot, weight_back, preferred_element_type=jnp.float32)]
    all_to_all x3 -> x1, waiting for transfers between devices: 0.01 us -> 66.6 us  [per_device(): lax.all_to_all(blocks, 'space', split_axis=0, concat_axis=0, tiled=True)]
    scatter-add x64 -> x0, local copies, waits for them, and re-layouts: 57.4 us -> none
    all_to_all x0 -> x1, blocking collectives: none -> 54.3 us  [per_device(): lax.all_to_all(reply.reshape(NY, NZ * CAP, 128), 'space', split_axis=0, c...]
  transfers between devices with their start and end apart: 4 -> 1, of which waited for: 1 -> 1; matrix products, arithmetic and copies ran while one was open for 46% -> 1% of each run, Pallas kernels for 0% -> 9%
where the time goes in v1:
time: 323 us; the launch traced here: 318 us
  Pallas kernels  181 us (56%)
  waiting for transfers between devices  66.6 us (21%)
  blocking collectives  54.3 us (17%)
  local copies, waits for them, and re-layouts  6.18 us (2%)
  starting transfers between devices  5.08 us (2%)
  other arithmetic  3.98 us (1%)
    all_to_all x1, waiting for transfers between devices, per_device(): lax.all_to_all(blocks, 'space', split_axis=0, concat_axis=0, tiled=True)  66.6 us
    pallas_call x1, Pallas kernels, exchange(): pl.pallas_call(exchange_kernel, out_shape=(jax.ShapeDtypeStruct((NZ, PAR,...  56.2 us
    all_to_all x1, blocking collectives, per_device(): lax.all_to_all(reply.reshape(NY, NZ * CAP, 128), 'space', split_axis=0, c...  54.3 us
    pallas_call x1, Pallas kernels, total(): pl.pallas_call(lambda *refs: total_kernel(scale, *refs), out_shape=jax.Sh...  31.4 us
    pallas_call x1, Pallas kernels, owner(): pl.pallas_call(owner_kernel, out_shape=(jax.ShapeDtypeStruct((PAR, 128),...  30.2 us
    pallas_call x1, Pallas kernels, fine(): pl.pallas_call(fine_kernel, out_shape=jax.ShapeDtypeStruct((rows, 128), B...  27.1 us
    pallas_call x1, Pallas kernels, gather(): pl.pallas_call(gather_kernel, out_shape=jax.ShapeDtypeStruct((NS, CAP, 12...  23.2 us
    pallas_call x1, Pallas kernels, pack(): pl.pallas_call(pack_kernel, out_shape=(jax.ShapeDtypeStruct((NS, CAP, 128...  12.7 us
  transfers between devices with their start and end apart: 1, of which 1 were waited for; matrix products, arithmetic and copies ran while one was open for 1% of the time, Pallas kernels for 9%

profile of v1, /device:TPU:2, one launch (start us, length us, event | category | flops | bytes accessed | tf_op | source)
XLA Modules:
  0.0 317.6 jit_solution(4743271484624438856)
XLA Ops:
  0.6 0.8 add_select_fusion
  1.4 0.2 convert_reduce_fusion
  1.6 0.7 fusion.4
  2.3 0.7 fusion.3.lo_ref
  3.0 0.8 broadcast_multiply_fusion
  3.7 0.8 negate_select_fusion
  4.5 0.6 pad.8.row_ref
  5.1 0.6 pad.7.slot_ref
  5.8 0.0 copy-done.2
  5.8 12.7 %pack.1 = (bf16[32,528,128]{2,1,0:T(8,128)(2,1)}, s32[32,8,128]{2,1,0:T(8,128)}, s32[32,8,128]{2,1,0:T(8,128)}) custom-call(s32[32]{0:T(128)} %copy-done.2, s32[32]{0:T(128)} %fusion.3.lo_ref, s32[32]{0:T(128)} %get-tuple-element.19.hi_ref, bf16[8192,128]{1,0:T(8,128)(2,1)} %bitcast.23, s32[80,128]{1,0:T(8,128)} %pad.7.slot_ref, s32[80,128]{1,0:T(8,128)} %pad.8.row_ref), custom_call_target="tpu_custom_call" | custom-call | tf_op jit(solution)/shard_map/pack/pallas_call | solution.py:47
  18.5 56.2 %exchange.1 = (bf16[8,2048,128]{2,1,0:T(8,128)(2,1)}, s32[4,64,128]{2,1,0:T(8,128)}, s32[32,8,128]{2,1,0:T(8,128)}) custom-call(bf16[2048,128]{1,0:T(8,128)(2,1)} %bitcast.21, s32[4,64,128]{2,1,0:T(8,128)} %bitcast.32, s32[32,8,128]{2,1,0:T(8,128)} %get-tuple-element.12.slots_ref), custom_call_target="tpu_custom_call" | custom-call | tf_op jit(solution)/shard_map/exchange/pallas_call | solution.py:152
  74.7 23.2 %gather.1 = bf16[32,528,128]{2,1,0:T(8,128)(2,1)} custom-call(s32[32768]{0:T(1024)} %bitcast.27, bf16[16384,128]{1,0:T(8,128)(2,1)} %bitcast.19), custom_call_target="tpu_custom_call" | custom-call | tf_op jit(solution)/shard_map/gather/pallas_call | solution.py:201
  97.9 54.3 %all_to_all.10 = bf16[4,4224,128]{2,1,0:T(8,128)(2,1)} all-to-all(bf16[4,4224,128]{2,1,0:T(8,128)(2,1)} %bitcast.18), channel_id=1, replica_groups={{0,8,16,24},{1,9,17,25},{2,10,18,26},{3,11,19,27},{4,12,20,28},{5,13,21..., dimensions={0} | all-to-all | bytes 8650752 | tf_op jit(solution)/shard_map/all_to_all | solution.py:421
  152.1 5.1 %all-to-all-start = ((bf16[32,528,128]{2,1,0:T(8,128)(2,1)}), bf16[32,528,128]{2,1,0:T(8,128)(2,1)}, u32[]{:S(2)}, u32[]{:S(2)}) async-start(bf16[32,528,128]{2,1,0:T(8,128)(2,1)} %get-tuple-element.14), calls=%async_computation | async-start | bytes 8650752 | tf_op jit(solution)/shard_map/all_to_all | solution.py:417
  157.2 0.0 copy-done
  157.2 0.9 copy.9
  158.1 0.0 copy-done.1
  158.1 0.1 convert_reduce_fusion.1
  158.2 2.2 broadcast_in_dim.14.kind_ref
  160.4 27.1 %fine.1 = bf16[8192,128]{1,0:T(8,128)(2,1)} custom-call(s32[32]{0:T(128)} %copy-done.2, s32[32]{0:T(128)} %fusion.3.lo_ref, s32[32]{0:T(128)} %get-tuple-element.19.hi_ref, bf16[32,528,128]{2,1,0:T(8,128)(2,1)} %bitcast.17, bf16[8192,128]{1,0:T(8,128)(2,1)} %broadcast_in_dim.14.kind_ref, bf16[1024,128]{1,0:T(8,128)(2,1)} %bitcast.26), custom_call_target="tpu_custom_call" | custom-call | tf_op jit(solution)/shard_map/fine/pallas_call | solution.py:386
  187.5 66.6 %all-to-all-done.blk_ref = bf16[32,528,128]{2,1,0:T(8,128)(2,1)} async-done(((bf16[32,528,128]{2,1,0:T(8,128)(2,1)}), bf16[32,528,128]{2,1,0:T(8,128)(2,1)}, u32[]{:S(2)}, u32[]{:S(2)}) %all-to-all-start) | async-done | bytes 4325408 | tf_op jit(solution)/shard_map/all_to_all | solution.py:417
  254.2 30.2 %owner.1 = (bf16[2048,128]{1,0:T(8,128)(2,1)}, f32[1024,128]{1,0:T(8,128)}) custom-call(s32[32768]{0:T(1024)} %bitcast.28, bf16[32,528,128]{2,1,0:T(8,128)(2,1)} %all-to-all-done.blk_ref, bf16[8,128,128]{2,1,0:T(8,128)(2,1)} %weight_ref.1, bf16[2048,128]{1,0:T(8,128)(2,1)} %bitcast.22), custom_call_target="tpu_custom_call" | custom-call | tf_op jit(solution)/shard_map/owner/pallas_call | solution.py:257
  284.3 31.4 %total.1 = f32[1024,128]{1,0:T(8,128)} custom-call(f32[1024,128]{1,0:T(8,128)} %get-tuple-element.18.refs_0_), custom_call_target="tpu_custom_call" | custom-call | tf_op jit(solution)/shard_map/total/pallas_call | solution.py:333
  315.7 1.9 copy.11
  (3 shorter events, 0.0 us)
Async XLA Ops:
  2.3 3.5 %copy-start.2 = (s32[32]{0:T(128)}, s32[32]{0:T(128)S(1)}, u32[]{:S(2)}) copy-start(s32[32]{0:T(128)S(1)} %get-tuple-element.20.first_ref) | copy-start | bytes 388
  152.1 5.1 %copy-start = (bf16[8,128,128]{2,1,0:T(8,128)(2,1)S(1)}, bf16[8,128,128]{2,1,0:T(8,128)(2,1)}, u32[]{:S(2)}) copy-start(bf16[8,128,128]{2,1,0:T(8,128)(2,1)} %weight_ref.1) | copy-start | bytes 786436
  152.1 6.0 %copy-start.1 = (s32[1,8192]{1,0:T(1,128)S(1)}, s32[1,8192]{1,0:T(1,128)}, u32[]{:S(2)}) copy-start(s32[1,8192]{1,0:T(1,128)} %param.7) | copy-start | bytes 98308
  152.1 102.0 %all-to-all-start = ((bf16[32,528,128]{2,1,0:T(8,128)(2,1)}), bf16[32,528,128]{2,1,0:T(8,128)(2,1)}, u32[]{:S(2)}, u32[]{:S(2)}) async-start(bf16[32,528,128]{2,1,0:T(8,128)(2,1)} %get-tuple-element.14), calls=%async_computation | async-start | bytes 8650752 | tf_op jit(solution)/shard_map/all_to_all | solution.py:417
